TPU v7x, 32 devices: a whole 2x2x4 slice. The times are simulated.
32 devices in a mesh: phys: 4 (over y, x), row: 2 (over core), col: 4 (over z).
Axes of the slice: x: 2, y: 2, z: 4, core: 2. Of those that a mesh axis runs over, the one named last changes fastest.
Arguments:
- rho_sites: bfloat16 [1, 16, 2048, 2048], P(None, 'phys', 'row', 'col'), may hold values from -0.0625 to 0.0625
- sigma_sites: bfloat16 [1, 16, 2048, 2048], P(None, 'phys', 'row', 'col'), may hold values from -0.0625 to 0.0625
- environment: float32 [2048, 2048], P('row', 'col'), may hold values from -6 to 6
Outputs:
- new_environment: float32 [2048, 2048], P('row', 'col')
All inputs are finite; a program needn't handle non-finite values.
Results may differ from a plain program's by a relative error of at most 0.004.
Values may be sent and summed in bfloat16 or wider, within the bound.
A program may use at most 128 MiB of HBM per device.

v0:
```python
import jax
import jax.numpy as jnp
from jax import lax
from jax.sharding import PartitionSpec as P


def per_device(rho_sites, sigma_sites, environment):
    env = environment
    rho_block = rho_sites[0]
    sigma_block = sigma_sites[0]
    env_b = env.astype(jnp.bfloat16)
    env_whole = lax.all_gather(env_b, "col", axis=1, tiled=True)
    half = jnp.einsum(
        "ik,pkl->pil",
        env_whole,
        lax.all_gather(sigma_block, "row", axis=1, tiled=True),
        preferred_element_type=jnp.float32,
    ).astype(jnp.bfloat16)
    partial_env = jnp.einsum(
        "pij,pil->jl",
        lax.all_gather(rho_block, "col", axis=2, tiled=True),
        half,
        preferred_element_type=jnp.float32,
    )
    row_part = lax.psum_scatter(partial_env, "row", scatter_dimension=0, tiled=True)
    env = lax.psum(row_part, "phys")
    return env


def solution(mesh):
    placed = (P(None, "phys", "row", "col"), P(None, "phys", "row", "col"), P("row", "col"))
    return jax.shard_map(
        per_device, mesh=mesh, in_specs=placed, out_specs=P("row", "col"), check_vma=False
    )
```

profile of v0, /device:TPU:0, one launch (start us, length us, event | category | flops | bytes accessed | tf_op | source)
XLA Modules:
  0.0 524.7 jit_solution(5357533425166158105)
XLA Ops:
  6.5 0.0 all-gather.6.cloned.1.call-start
  6.5 2.7 convert_element_type.9
  9.2 0.0 all-gather.6.cloned.1.call-update
  9.3 0.0 all-gather.8.cloned.1.call-start
  9.3 0.7 all-gather.8.cloned.1.call-update
  10.0 0.0 all-gather.10.cloned.1.call-start
  10.1 0.7 all-gather.10.cloned.1.call-update
  10.7 0.0 reduce-scatter.2.cloned.1.call-start
  10.8 82.1 %all-gather.6.cloned.1.call-done = bf16[1024,2048]{1,0:T(8,128)(2,1)} async-done(((bf16[1024,512]{1,0:T(8,128)(2,1)}), bf16[1024,2048]{1,0:T(8,128)(2,1)}) %all-gather.6.cloned.1.call-update) | async-done | bytes 4194320 | tf_op jit(solution)/shard_map/all_gather | solution.py:12
  92.9 19.9 %all-gather.8.cloned.1.call-done = bf16[1,4,2048,512]{3,2,1,0:T(8,128)(2,1)} async-done(((bf16[1,4,1024,512]{3,2,1,0:T(8,128)(2,1)}), bf16[1,4,2048,512]{3,2,1,0:T(8,128)(2,1)}) %all-gather.8.cloned.1.call-update) | async-done | bytes 8388624 | tf_op jit(solution)/shard_map/all_gather | solution.py:16
  112.8 289.5 %all-gather.10.cloned.1.call-done = bf16[1,4,1024,2048]{3,2,1,0:T(8,128)(2,1)} async-done(((bf16[1,4,1024,512]{3,2,1,0:T(8,128)(2,1)}), bf16[1,4,1024,2048]{3,2,1,0:T(8,128)(2,1)}) %all-gather.10.cloned.1.call-update) | async-done | bytes 16777232 | tf_op jit(solution)/shard_map/all_gather | solution.py:21
  402.3 29.0 %fusion.15 = f32[2048,512]{0,1:T(8,128)} fusion(bf16[1,4,1024,2048]{3,2,1,0:T(8,128)(2,1)} %all-gather.10.cloned.1.call-done, bf16[1024,2048]{1,0:T(8,128)(2,1)} %all-gather.6.cloned.1.call-done, bf16[1,4,2048,512]{3,2,1,0:T(8,128)(2,1)} %all-gather.8.cloned.1.call-done), kind=kOutput, calls=%fused_computation.7 | convolution fusion | flops 17181966336 | bytes 33554432 | tf_op jit(solution)/shard_map/pij,pil->jl/dot_general | solution.py:19
  431.3 0.0 reduce-scatter.2.cloned.1.call-update
  431.3 0.0 all-reduce.2.cloned.1.call-start
  431.4 10.2 %reduce-scatter.2.cloned.1.call-done = f32[1024,512]{0,1:T(8,128)} async-done(((f32[2048,512]{0,1:T(8,128)}), f32[1024,512]{0,1:T(8,128)}) %reduce-scatter.2.cloned.1.call-update) | async-done | bytes 2097168 | tf_op jit(solution)/shard_map/reduce_scatter | solution.py:25
  441.6 0.0 all-reduce.2.cloned.1.call-update
  441.6 73.7 %all-reduce.2.cloned.1.call-done = f32[1024,512]{0,1:T(8,128)} async-done(((f32[1024,512]{0,1:T(8,128)}), f32[1024,512]{0,1:T(8,128)}) %all-reduce.2.cloned.1.call-update) | async-done | bytes 2097168 | tf_op jit(solution)/shard_map/psum | solution.py:26
  515.3 2.9 copy.4
Async XLA Ops:
  6.5 86.3 %all-gather.6.cloned.1.call-start = ((), (), s32[]{:S(2)}) async-start(), calls=%async_computation.1 | async-start | bytes 5242880 | tf_op jit(solution)/shard_map/all_gather | solution.py:12
  9.3 103.5 %all-gather.8.cloned.1.call-start = ((), (), s32[]{:S(2)}) async-start(), calls=%async_computation.4 | async-start | bytes 12582912 | tf_op jit(solution)/shard_map/all_gather | solution.py:16
  10.0 392.3 %all-gather.10.cloned.1.call-start = ((), (), s32[]{:S(2)}) async-start(), calls=%async_computation.5 | async-start | bytes 20971520 | tf_op jit(solution)/shard_map/all_gather | solution.py:21
  10.7 430.8 %reduce-scatter.2.cloned.1.call-start = ((), (), s32[]{:S(2)}) async-start(), calls=%async_computation.2 | async-start | bytes 6291456 | tf_op jit(solution)/shard_map/reduce_scatter | solution.py:25
  431.3 84.0 %all-reduce.2.cloned.1.call-start = ((), (), s32[]{:S(2)}) async-start(), calls=%async_computation.3 | async-start | bytes 4194304 | tf_op jit(solution)/shard_map/psum | solution.py:26
Sparse Core Ops, SparseCore 0:
  9.4 83.4 all-gather.5
  94.4 18.3 all-gather.7
  114.4 287.9 all-gather.9
  431.5 10.0 reduce-scatter.1
  444.5 70.7 all-reduce.1
where the time goes:
time: 525 us
  waiting for transfers between devices  477 us (91%)
  matrix products  29 us (6%)
  between operations  13.1 us (2%)
    all_gather x1, waiting for transfers between devices, per_device(): lax.all_gather(rho_block, 'col', axis=2, tiled=True)  290 us
    all_gather x1, waiting for transfers between devices, per_device(): env_whole = lax.all_gather(env_b, 'col', axis=1, tiled=True)  82.1 us
    psum x1, waiting for transfers between devices, per_device(): env = lax.psum(row_part, 'phys')  73.7 us
    dot_general x1, matrix products, per_device(): jnp.einsum('pij,pil->jl', lax.all_gather(rho_block, 'col', axis=2, tiled=...  29 us
    all_gather x1, waiting for transfers between devices, per_device(): lax.all_gather(sigma_block, 'row', axis=1, tiled=True)  19.9 us
  transfers between devices with their start and end apart: 5, of which 5 were waited for; matrix products, arithmetic and copies ran while one was open for 0% of the time, Pallas kernels for 0%

commit v1 on v0

--- a/solution.py
+++ b/solution.py
@@ -23,7 +23,9 @@
         preferred_element_type=jnp.float32,
     )
     row_part = lax.psum_scatter(partial_env, "row", scatter_dimension=0, tiled=True)
-    env = lax.psum(row_part, "phys")
+    env = row_part
+    for hop in (1, 2):
+        env = env + lax.ppermute(env, "phys", [(dev, dev ^ hop) for dev in range(4)])
     return env
 
 

time: 525 us -> 548 us (1.044)
  waiting for transfers between devices: 477 us -> 495 us
    ppermute x0 -> x2, waiting for transfers between devices: none -> 91.5 us  [per_device(): lax.ppermute(env, 'phys', [(dev, dev ^ hop) for dev in range(4)])]
    psum x1 -> x0, waiting for transfers between devices: 73.7 us -> none  [per_device(): env = lax.psum(row_part, 'phys')]
  transfers between devices with their start and end apart: 5 -> 6, of which waited for: 5 -> 6; matrix products, arithmetic and copies ran while one was open for 0% -> 0% of each run, Pallas kernels for 0% -> 0%
where the time goes in v1:
time: 548 us
  waiting for transfers between devices  495 us (90%)
  matrix products  29.2 us (5%)
  between operations  13.1 us (2%)
    all_gather x1, waiting for transfers between devices, per_device(): lax.all_gather(rho_block, 'col', axis=2, tiled=True)  290 us
    ppermute x2, waiting for transfers between devices, per_device(): lax.ppermute(env, 'phys', [(dev, dev ^ hop) for dev in range(4)])  91.5 us
    all_gather x1, waiting for transfers between devices, per_device(): env_whole = lax.all_gather(env_b, 'col', axis=1, tiled=True)  82.1 us
    dot_general x1, matrix products, per_device(): jnp.einsum('pij,pil->jl', lax.all_gather(rho_block, 'col', axis=2, tiled=...  29.2 us
    all_gather x1, waiting for transfers between devices, per_device(): lax.all_gather(sigma_block, 'row', axis=1, tiled=True)  19.9 us
  transfers between devices with their start and end apart: 6, of which 6 were waited for; matrix products, arithmetic and copies ran while one was open for 0% of the time, Pallas kernels for 0%

profile of v1, /device:TPU:0, one launch (start us, length us, event | category | flops | bytes accessed | tf_op | source)
XLA Modules:
  0.0 547.6 jit_solution(5187695963952920396)
XLA Ops:
  6.5 0.0 all-gather.6.cloned.1.call-start
  6.5 2.7 convert_element_type.9
  9.2 0.0 all-gather.6.cloned.1.call-update
  9.3 0.0 all-gather.8.cloned.1.call-start
  9.3 0.7 all-gather.8.cloned.1.call-update
  10.0 0.0 all-gather.10.cloned.1.call-start
  10.1 0.7 all-gather.10.cloned.1.call-update
  10.7 0.0 reduce-scatter.2.cloned.1.call-start
  10.8 82.1 %all-gather.6.cloned.1.call-done = bf16[1024,2048]{1,0:T(8,128)(2,1)} async-done(((bf16[1024,512]{1,0:T(8,128)(2,1)}), bf16[1024,2048]{1,0:T(8,128)(2,1)}) %all-gather.6.cloned.1.call-update) | async-done | bytes 4194320 | tf_op jit(solution)/shard_map/all_gather | solution.py:12
  92.9 19.9 %all-gather.8.cloned.1.call-done = bf16[1,4,2048,512]{3,2,1,0:T(8,128)(2,1)} async-done(((bf16[1,4,1024,512]{3,2,1,0:T(8,128)(2,1)}), bf16[1,4,2048,512]{3,2,1,0:T(8,128)(2,1)}) %all-gather.8.cloned.1.call-update) | async-done | bytes 8388624 | tf_op jit(solution)/shard_map/all_gather | solution.py:16
  112.8 289.5 %all-gather.10.cloned.1.call-done = bf16[1,4,1024,2048]{3,2,1,0:T(8,128)(2,1)} async-done(((bf16[1,4,1024,512]{3,2,1,0:T(8,128)(2,1)}), bf16[1,4,1024,2048]{3,2,1,0:T(8,128)(2,1)}) %all-gather.10.cloned.1.call-update) | async-done | bytes 16777232 | tf_op jit(solution)/shard_map/all_gather | solution.py:21
  402.3 29.2 %fusion.15 = f32[2048,512]{0,1:T(8,128)} fusion(bf16[1,4,1024,2048]{3,2,1,0:T(8,128)(2,1)} %all-gather.10.cloned.1.call-done, bf16[1024,2048]{1,0:T(8,128)(2,1)} %all-gather.6.cloned.1.call-done, bf16[1,4,2048,512]{3,2,1,0:T(8,128)(2,1)} %all-gather.8.cloned.1.call-done), kind=kOutput, calls=%fused_computation.7 | convolution fusion | flops 17181966336 | bytes 33554432 | tf_op jit(solution)/shard_map/pij,pil->jl/dot_general | solution.py:19
  431.5 0.0 reduce-scatter.2.cloned.1.call-update
  431.5 10.2 %reduce-scatter.2.cloned.1.call-done = f32[1024,512]{0,1:T(8,128)} async-done(((f32[2048,512]{0,1:T(8,128)}), f32[1024,512]{0,1:T(8,128)}) %reduce-scatter.2.cloned.1.call-update) | async-done | bytes 2097168 | tf_op jit(solution)/shard_map/reduce_scatter | solution.py:25
  441.8 1.8 collective-permute-start
  443.6 46.2 %collective-permute-done = f32[1024,512]{0,1:T(8,128)S(1)} collective-permute-done((f32[1024,512]{0,1:T(8,128)}, f32[1024,512]{0,1:T(8,128)S(1)}, u32[]{:S(2)}, u32[]{:S(2)}) %collective-permute-start) | collective-permute-done | bytes 2097184 | tf_op jit(solution)/shard_map/ppermute | solution.py:28
  489.8 2.0 add.8
  491.8 1.8 collective-permute-start.1
  493.6 45.3 %collective-permute-done.1 = f32[1024,512]{0,1:T(8,128)S(1)} collective-permute-done((f32[1024,512]{0,1:T(8,128)S(1)}, f32[1024,512]{0,1:T(8,128)S(1)}, u32[]{:S(2)}, u32[]{:S(2)}) %collective-permute-start.1) | collective-permute-done | bytes 2097184 | tf_op jit(solution)/shard_map/ppermute | solution.py:28
  538.9 0.4 add.9
  539.2 1.8 copy.4
Async XLA Ops:
  6.5 86.3 %all-gather.6.cloned.1.call-start = ((), (), s32[]{:S(2)}) async-start(), calls=%async_computation.1 | async-start | bytes 5242880 | tf_op jit(solution)/shard_map/all_gather | solution.py:12
  9.3 103.5 %all-gather.8.cloned.1.call-start = ((), (), s32[]{:S(2)}) async-start(), calls=%async_computation.3 | async-start | bytes 12582912 | tf_op jit(solution)/shard_map/all_gather | solution.py:16
  10.0 392.3 %all-gather.10.cloned.1.call-start = ((), (), s32[]{:S(2)}) async-start(), calls=%async_computation.4 | async-start | bytes 20971520 | tf_op jit(solution)/shard_map/all_gather | solution.py:21
  10.7 431.0 %reduce-scatter.2.cloned.1.call-start = ((), (), s32[]{:S(2)}) async-start(), calls=%async_computation.2 | async-start | bytes 6291456 | tf_op jit(solution)/shard_map/reduce_scatter | solution.py:25
  441.8 48.1 %collective-permute-start = (f32[1024,512]{0,1:T(8,128)}, f32[1024,512]{0,1:T(8,128)S(1)}, u32[]{:S(2)}, u32[]{:S(2)}) collective-permute-start(f32[1024,512]{0,1:T(8,128)} %reduce-scatter.2.cloned.1.call-done), channel_id=1, source_target_pairs={{0,8},{8,0},{16,24},{24,16},{1,9},{9,1},{17,25},{25,17},{2,10},{10... | collective-permute-start | bytes 6291464 | tf_op jit(solution)/shard_map/ppermute | solution.py:28
  491.8 47.1 %collective-permute-start.1 = (f32[1024,512]{0,1:T(8,128)S(1)}, f32[1024,512]{0,1:T(8,128)S(1)}, u32[]{:S(2)}, u32[]{:S(2)}) collective-permute-start(f32[1024,512]{0,1:T(8,128)S(1)} %add.8), channel_id=1, source_target_pairs={{0,16},{8,24},{16,0},{24,8},{1,17},{9,25},{17,1},{25,9},{2,18},{10... | collective-permute-start | bytes 6291464 | tf_op jit(solution)/shard_map/ppermute | solution.py:28
Sparse Core Ops, SparseCore 0:
  9.4 83.4 all-gather.5
  94.4 18.3 all-gather.7
  114.4 287.9 all-gather.9
  431.6 10.0 reduce-scatter.1
